TPU v7x, 32 devices: a whole 2x2x4 slice. The times are simulated.
32 devices in a mesh: fsdp: 4 (over x, core), tp: 8 (over z, y).
Axes of the slice: x: 2, y: 2, z: 4, core: 2. Of those that a mesh axis runs over, the one named last changes fastest.
Arguments:
- hidden_in: bfloat16 [8, 1024, 1024], P('fsdp', 'tp'), may hold values from -6 to 6
- grad_out: bfloat16 [8, 1024, 1024], P('fsdp', 'tp'), may hold values from -6 to 6
- condition: float32 [8, 1024], P('fsdp', 'tp'), may hold values from -6 to 6
- w_mod: bfloat16 [1024, 6144], P('tp', 'fsdp'), may hold values from -0.1875 to 0.1875
- b_mod: bfloat16 [6144], P('fsdp'), may hold values from -3 to 3
- w_qkv: bfloat16 [1024, 16, 192], P('fsdp', 'tp'), may hold values from -0.1875 to 0.1875
- b_qv: bfloat16 [16, 128], P('tp', 'fsdp'), may hold values from -2 to 2
- w_proj: bfloat16 [1024, 1024], P('tp', 'fsdp'), may hold values from -2 to 2
- b_proj: bfloat16 [1024], P('fsdp'), may hold values from -3 to 3
- w_fc1: bfloat16 [1024, 4096], P('fsdp', 'tp'), may hold values from -0.1875 to 0.1875
- b_fc1: bfloat16 [4096], P(('tp', 'fsdp')), may hold values from -3 to 3
- w_fc2: bfloat16 [4096, 1024], P('tp', 'fsdp'), may hold values from -0.375 to 0.375
- b_fc2: bfloat16 [1024], P('fsdp'), may hold values from -3 to 3
Outputs:
- block_out: float32 [8, 1024, 1024], P('fsdp', 'tp')
- grad_input: float32 [8, 1024, 1024], P('fsdp', 'tp')
- grad_cond: float32 [8, 1024], P('fsdp', 'tp')
- grad_w_mod: float32 [1024, 6144], P('tp', 'fsdp')
- grad_b_mod: float32 [6144], P('fsdp')
- grad_w_qkv: float32 [1024, 16, 192], P('fsdp', 'tp')
- grad_b_qv: float32 [16, 128], P('tp', 'fsdp')
- grad_w_proj: float32 [1024, 1024], P('tp', 'fsdp')
- grad_b_proj: float32 [1024], P('fsdp')
- grad_w_fc1: float32 [1024, 4096], P('fsdp', 'tp')
- grad_b_fc1: float32 [4096], P(('tp', 'fsdp'))
- grad_w_fc2: float32 [4096, 1024], P('tp', 'fsdp')
- grad_b_fc2: float32 [1024], P('fsdp')
All inputs are finite; a program needn't handle non-finite values.
Results may differ from a plain program's by a relative error of at most 0.013.
The roundings to bfloat16 on the way count: a program that leaves them out, or rounds other values in their place, can miss the bound.
Values may be sent and summed in bfloat16 or wider, within the bound.
No kernel may reach another device: no remote copies, remote signals or barrier semaphores. Data moves between devices by JAX's collectives and lax.ppermute only.
A program may use at most 128 MiB of HBM per device.

v0:
```python
import jax
import jax.numpy as jnp
from jax import lax
from jax.sharding import PartitionSpec as P

EPSILON = 1e-06


def layer_norm(values):
    center_mean = jnp.mean(values, -1, keepdims=True)
    centered = values - center_mean
    variance = jnp.mean(centered * centered, -1, keepdims=True)
    inv_std = lax.rsqrt(variance + EPSILON)
    return (centered * inv_std, inv_std)


def norm_back(grad_normed, normed, inv_std):
    return inv_std * (
        grad_normed
        - jnp.mean(grad_normed, -1, keepdims=True)
        - normed * jnp.mean(grad_normed * normed, -1, keepdims=True)
    )


def gelu_tanh(values):
    return jax.nn.gelu(values, approximate=True)


def piece_of(modulation, index, width):
    return modulation[:, None, index * width : (index + 1) * width]


def attend_one(items):
    query_rows, key_rows, value_rows = items
    score_scale = query_rows.shape[-1] ** (-0.5)
    scores = (
        jnp.einsum("qhe,khe->hqk", query_rows, key_rows, preferred_element_type=jnp.float32)
        * score_scale
    )
    row_max = jnp.max(scores, -1, keepdims=True)
    log_total = row_max + jnp.log(jnp.sum(jnp.exp(scores - row_max), -1, keepdims=True))
    probs_low = jnp.exp(scores - log_total).astype(jnp.bfloat16)
    attended = jnp.einsum("hqk,khe->qhe", probs_low, value_rows, preferred_element_type=jnp.float32)
    return (attended.astype(jnp.bfloat16), log_total)


def attend_back(items):
    query_rows, key_rows, value_rows, log_total, grad_attended = items
    score_scale = query_rows.shape[-1] ** (-0.5)
    scores = (
        jnp.einsum("qhe,khe->hqk", query_rows, key_rows, preferred_element_type=jnp.float32)
        * score_scale
    )
    probs = jnp.exp(scores - log_total)
    probs_low = probs.astype(jnp.bfloat16)
    grad_probs = jnp.einsum(
        "qhe,khe->hqk", grad_attended, value_rows, preferred_element_type=jnp.float32
    )
    inner = jnp.sum(probs * grad_probs, -1, keepdims=True)
    grad_scores = (probs * (grad_probs - inner)).astype(jnp.bfloat16)
    grad_query = (
        jnp.einsum("hqk,khe->qhe", grad_scores, key_rows, preferred_element_type=jnp.float32)
        * score_scale
    )
    grad_keys = (
        jnp.einsum("hqk,qhe->khe", grad_scores, query_rows, preferred_element_type=jnp.float32)
        * score_scale
    )
    grad_values = jnp.einsum(
        "hqk,qhe->khe", probs_low, grad_attended, preferred_element_type=jnp.float32
    )
    return jnp.concatenate([grad_query, grad_keys, grad_values], -1).astype(jnp.bfloat16)


def on_device(
    hidden_in,
    grad_out,
    condition,
    w_mod,
    b_mod,
    w_qkv,
    b_qv,
    w_proj,
    b_proj,
    w_fc1,
    b_fc1,
    w_fc2,
    b_fc2,
):
    latents = hidden_in.shape[0]
    width = hidden_in.shape[2]
    (
        mod_rows,
        mod_bias,
        qkv_cols,
        qv_bias,
        proj_rows,
        proj_bias,
        fc1_cols,
        fc1_bias,
        fc2_rows,
        fc2_bias,
    ) = (
        lax.all_gather(w_mod, "fsdp", axis=1, tiled=True),
        lax.all_gather(b_mod, "fsdp", axis=0, tiled=True),
        lax.all_gather(w_qkv, "fsdp", axis=0, tiled=True),
        lax.all_gather(b_qv, "fsdp", axis=1, tiled=True),
        lax.all_gather(w_proj, "fsdp", axis=1, tiled=True),
        lax.all_gather(b_proj, "fsdp", axis=0, tiled=True),
        lax.all_gather(w_fc1, "fsdp", axis=0, tiled=True),
        lax.all_gather(b_fc1, "fsdp", axis=0, tiled=True),
        lax.all_gather(w_fc2, "fsdp", axis=1, tiled=True),
        lax.all_gather(b_fc2, "fsdp", axis=0, tiled=True),
    )
    heads_here = qkv_cols.shape[1]
    head_dim = qkv_cols.shape[2] // 3
    cond_act, silu_back = jax.vjp(jax.nn.silu, condition)
    cond_low = cond_act.astype(jnp.bfloat16)
    modulation = lax.psum(
        jnp.dot(cond_low, mod_rows, preferred_element_type=jnp.float32), "tp"
    ) + mod_bias.astype(jnp.float32)
    shift_one = piece_of(modulation, 0, width)
    scale_one = piece_of(modulation, 1, width)
    gate_one = piece_of(modulation, 2, width)
    shift_two = piece_of(modulation, 3, width)
    scale_two = piece_of(modulation, 4, width)
    gate_two = piece_of(modulation, 5, width)
    resid_in = hidden_in.astype(jnp.float32)
    normed_one, inv_one = layer_norm(resid_in)
    attn_local = (normed_one * (1.0 + scale_one) + shift_one).astype(jnp.bfloat16)
    attn_rows = lax.all_gather(attn_local, "tp", axis=1, tiled=True)
    seq_len = attn_rows.shape[1]
    total_rows = latents * seq_len
    qkv_matrix = qkv_cols.reshape(width, heads_here * 3 * head_dim)
    qv_float = qv_bias.astype(jnp.float32)
    bias_three = jnp.concatenate(
        [
            qv_float[:, :head_dim],
            jnp.zeros((heads_here, head_dim), jnp.float32),
            qv_float[:, head_dim:],
        ],
        -1,
    )
    projected = (
        jnp.dot(
            attn_rows.reshape(total_rows, width), qkv_matrix, preferred_element_type=jnp.float32
        ).reshape(latents, seq_len, heads_here, 3 * head_dim)
        + bias_three
    ).astype(jnp.bfloat16)
    query_rows = projected[..., :head_dim]
    key_rows = projected[..., head_dim : 2 * head_dim]
    value_rows = projected[..., 2 * head_dim :]
    attended, log_total = lax.map(attend_one, (query_rows, key_rows, value_rows))
    attended_flat = attended.reshape(total_rows, heads_here * head_dim)
    attn_terms = jnp.dot(attended_flat, proj_rows, preferred_element_type=jnp.float32).reshape(
        latents, seq_len, width
    )
    attn_sums = lax.psum_scatter(attn_terms, "tp", scatter_dimension=1, tiled=True)
    attn_branch = attn_sums + proj_bias.astype(jnp.float32)
    resid_mid = resid_in + gate_one * attn_branch
    normed_two, inv_two = layer_norm(resid_mid)
    mlp_local = (normed_two * (1.0 + scale_two) + shift_two).astype(jnp.bfloat16)
    mlp_rows = lax.all_gather(mlp_local, "tp", axis=1, tiled=True)
    pre_act = jnp.dot(
        mlp_rows.reshape(total_rows, width), fc1_cols, preferred_element_type=jnp.float32
    ) + fc1_bias.astype(jnp.float32)
    act_float, gelu_back = jax.vjp(gelu_tanh, pre_act)
    act_low = act_float.astype(jnp.bfloat16)
    mlp_terms = jnp.dot(act_low, fc2_rows, preferred_element_type=jnp.float32).reshape(
        latents, seq_len, width
    )
    mlp_branch = lax.psum_scatter(
        mlp_terms, "tp", scatter_dimension=1, tiled=True
    ) + fc2_bias.astype(jnp.float32)
    block_out = resid_mid + gate_two * mlp_branch
    cotangent = grad_out.astype(jnp.float32)
    grad_gate_two = jnp.sum(cotangent * mlp_branch, 1)
    grad_mlp_out = (gate_two * cotangent).astype(jnp.bfloat16)
    grad_mlp_rows = lax.all_gather(grad_mlp_out, "tp", axis=1, tiled=True).reshape(
        total_rows, width
    )
    grad_fc2 = jnp.dot(act_low.T, grad_mlp_rows, preferred_element_type=jnp.float32)
    grad_fc2_bias = jnp.sum(grad_mlp_rows.astype(jnp.float32), 0)
    grad_act = jnp.dot(grad_mlp_rows, fc2_rows.T, preferred_element_type=jnp.float32)
    grad_pre = gelu_back(grad_act)[0].astype(jnp.bfloat16)
    grad_fc1 = jnp.dot(
        mlp_rows.reshape(total_rows, width).T, grad_pre, preferred_element_type=jnp.float32
    )
    grad_fc1_bias = jnp.sum(grad_pre.astype(jnp.float32), 0)
    mlp_in_terms = jnp.dot(grad_pre, fc1_cols.T, preferred_element_type=jnp.float32).reshape(
        latents, seq_len, width
    )
    grad_mlp_in = lax.psum_scatter(mlp_in_terms, "tp", scatter_dimension=1, tiled=True)
    grad_scale_two = jnp.sum(grad_mlp_in * normed_two, 1)
    grad_shift_two = jnp.sum(grad_mlp_in, 1)
    grad_mid = cotangent + norm_back(grad_mlp_in * (1.0 + scale_two), normed_two, inv_two)
    grad_gate_one = jnp.sum(grad_mid * attn_branch, 1)
    grad_attn_out = (gate_one * grad_mid).astype(jnp.bfloat16)
    grad_attn_rows = lax.all_gather(grad_attn_out, "tp", axis=1, tiled=True).reshape(
        total_rows, width
    )
    grad_proj = jnp.dot(attended_flat.T, grad_attn_rows, preferred_element_type=jnp.float32)
    grad_proj_bias = jnp.sum(grad_attn_rows.astype(jnp.float32), 0)
    grad_attended = (
        jnp.dot(grad_attn_rows, proj_rows.T, preferred_element_type=jnp.float32)
        .astype(jnp.bfloat16)
        .reshape(latents, seq_len, heads_here, head_dim)
    )
    grad_projected = lax.map(
        attend_back, (query_rows, key_rows, value_rows, log_total, grad_attended)
    )
    grad_flat = grad_projected.reshape(total_rows, heads_here * 3 * head_dim)
    grad_qkv = jnp.dot(
        attn_rows.reshape(total_rows, width).T, grad_flat, preferred_element_type=jnp.float32
    ).reshape(width, heads_here, 3 * head_dim)
    bias_sums = jnp.sum(grad_projected.astype(jnp.float32), (0, 1))
    grad_qv_bias = jnp.concatenate([bias_sums[:, :head_dim], bias_sums[:, 2 * head_dim :]], -1)
    attn_in_terms = jnp.dot(grad_flat, qkv_matrix.T, preferred_element_type=jnp.float32).reshape(
        latents, seq_len, width
    )
    grad_attn_in = lax.psum_scatter(attn_in_terms, "tp", scatter_dimension=1, tiled=True)
    grad_scale_one = jnp.sum(grad_attn_in * normed_one, 1)
    grad_shift_one = jnp.sum(grad_attn_in, 1)
    grad_input = grad_mid + norm_back(grad_attn_in * (1.0 + scale_one), normed_one, inv_one)
    mod_terms = jnp.concatenate(
        [
            grad_shift_one,
            grad_scale_one,
            grad_gate_one,
            grad_shift_two,
            grad_scale_two,
            grad_gate_two,
        ],
        -1,
    )
    grad_modulation = lax.psum(mod_terms, "tp")
    grad_mod_low = grad_modulation.astype(jnp.bfloat16)
    grad_mod_w = jnp.dot(cond_low.T, grad_mod_low, preferred_element_type=jnp.float32)
    grad_mod_bias = jnp.sum(grad_modulation, 0)
    grad_cond = silu_back(jnp.dot(grad_mod_low, mod_rows.T, preferred_element_type=jnp.float32))[0]
    owned = (
        lax.psum_scatter(grad_mod_w, "fsdp", scatter_dimension=1, tiled=True),
        lax.psum_scatter(grad_mod_bias, "fsdp", scatter_dimension=0, tiled=True),
        lax.psum_scatter(grad_qkv, "fsdp", scatter_dimension=0, tiled=True),
        lax.psum_scatter(grad_qv_bias, "fsdp", scatter_dimension=1, tiled=True),
        lax.psum_scatter(grad_proj, "fsdp", scatter_dimension=1, tiled=True),
        lax.psum_scatter(grad_proj_bias, "fsdp", scatter_dimension=0, tiled=True),
        lax.psum_scatter(grad_fc1, "fsdp", scatter_dimension=0, tiled=True),
        lax.psum_scatter(grad_fc1_bias, "fsdp", scatter_dimension=0, tiled=True),
        lax.psum_scatter(grad_fc2, "fsdp", scatter_dimension=1, tiled=True),
        lax.psum_scatter(grad_fc2_bias, "fsdp", scatter_dimension=0, tiled=True),
    )
    return (
        block_out,
        grad_input,
        grad_cond,
        owned[0],
        owned[1],
        owned[2],
        owned[3],
        owned[4],
        owned[5],
        owned[6],
        owned[7],
        owned[8],
        owned[9],
    )


def solution(mesh):
    placed = (
        P("fsdp", "tp", None),
        P("fsdp", "tp", None),
        P("fsdp", "tp"),
        P("tp", "fsdp"),
        P("fsdp"),
        P("fsdp", "tp", None),
        P("tp", "fsdp"),
        P("tp", "fsdp"),
        P("fsdp"),
        P("fsdp", "tp"),
        P(("tp", "fsdp")),
        P("tp", "fsdp"),
        P("fsdp"),
    )
    return jax.shard_map(
        on_device,
        mesh=mesh,
        in_specs=placed,
        out_specs=(
            P("fsdp", "tp", None),
            P("fsdp", "tp", None),
            P("fsdp", "tp"),
            P("tp", "fsdp"),
            P("fsdp"),
            P("fsdp", "tp", None),
            P("tp", "fsdp"),
            P("tp", "fsdp"),
            P("fsdp"),
            P("fsdp", "tp"),
            P(("tp", "fsdp")),
            P("tp", "fsdp"),
            P("fsdp"),
        ),
        check_vma=False,
    )
```

profile of v0, /device:TPU:0, one launch (start us, length us, event | category | flops | bytes accessed | tf_op | source)
XLA Modules:
  0.0 1253.0 jit_solution(13203060806068812908)
XLA Ops:
  8.7 6.2 all-gather
  17.5 14.5 %all-gather.13.cloned.1.call-done = bf16[128,6144]{1,0:T(8,128)(2,1)} async-done(((bf16[128,1536]{1,0:T(8,128)(2,1)}), bf16[128,6144]{1,0:T(8,128)(2,1)}) %all-gather.13.cloned.1.call-update) | async-done | bytes 1572880 | tf_op jit(solution)/shard_map/all_gather | solution.py:104
  32.0 1.7 fusion.88
  33.7 37.5 %psum.14 = f32[2,6144]{1,0:T(2,128)S(1)} all-reduce(f32[2,6144]{1,0:T(2,128)S(1)} %fusion.88), channel_id=1, replica_groups=mesh['fsdp'=4,'tp'=8] {'tp'}, use_global_device_ids=true, to_apply=%region_0.1 | all-reduce | flops 12288 | bytes 98304 | tf_op jit(solution)/shard_map/psum | solution.py:119
  71.9 2.1 fusion.67
  74.1 5.1 all-gather.1
  79.4 5.8 all_gather.47
  85.3 8.7 all_gather.45
  94.0 49.3 %all-gather.15.cloned.1.call-done = bf16[2,1024,1024]{2,1,0:T(8,128)(2,1)} async-done(((bf16[2,128,1024]{2,1,0:T(8,128)(2,1)}), bf16[2,1024,1024]{2,1,0:T(8,128)(2,1)}) %all-gather.15.cloned.1.call-update) | async-done | bytes 4194320 | tf_op jit(solution)/shard_map/all_gather | solution.py:131
  143.3 4.0 add_convert_fusion
  147.5 8.6 while.22
  148.8 1.4 exponential_reduce_fusion.2
  150.2 1.5 fusion.139
  153.1 1.4 exponential_reduce_fusion.2
  154.5 1.5 fusion.139
  156.0 4.5 fusion.78
  161.2 5.1 all-gather.2
  166.3 140.4 %reduce-scatter.13.cloned.1.call-done = f32[2,128,1024]{2,1,0:T(8,128)} async-done(((f32[2,1024,1024]{2,1,0:T(8,128)}), f32[2,128,1024]{2,1,0:T(8,128)}) %reduce-scatter.13.cloned.1.call-update) | async-done | bytes 1048592 | tf_op jit(solution)/shard_map/reduce_scatter | solution.py:158
  306.7 1.5 fusion.92
  310.2 2.0 fusion.74
  312.2 5.2 all-gather.3
  317.5 6.5 all-gather.19.cloned.1.call-done
  323.9 75.4 %all-gather.17.cloned.1.call-done = bf16[2,1024,1024]{2,1,0:T(8,128)(2,1)} async-done(((bf16[2,128,1024]{2,1,0:T(8,128)(2,1)}), bf16[2,1024,1024]{2,1,0:T(8,128)(2,1)}) %all-gather.17.cloned.1.call-update) | async-done | bytes 4194320 | tf_op jit(solution)/shard_map/all_gather | solution.py:163
  399.4 6.8 fusion.97
  406.1 10.0 all-gather.21.cloned.1.call-done
  416.2 75.6 %all-gather.23.cloned.1.call-done = bf16[2,1024,1024]{2,1,0:T(8,128)(2,1)} async-done(((bf16[2,128,1024]{2,1,0:T(8,128)(2,1)}), bf16[2,1024,1024]{2,1,0:T(8,128)(2,1)}) %all-gather.23.cloned.1.call-update) | async-done | bytes 4194320 | tf_op jit(solution)/shard_map/all_gather | solution.py:179
  491.7 9.0 convert_reduce_fusion.2
  500.7 5.6 fusion.98
  506.4 8.6 fusion.90
  515.6 5.1 all-gather.4
  520.7 131.8 %reduce-scatter.17.cloned.1.call-done = f32[2,128,1024]{2,1,0:T(8,128)} async-done(((f32[2,1024,1024]{2,1,0:T(8,128)}), f32[2,128,1024]{2,1,0:T(8,128)}) %reduce-scatter.17.cloned.1.call-update) | async-done | bytes 1048592 | tf_op jit(solution)/shard_map/reduce_scatter | solution.py:193
  652.5 1.7 multiply_reduce_fusion.2
  654.3 148.5 %reduce-scatter.15.cloned.1.call-done = f32[2,128,1024]{2,1,0:T(8,128)} async-done(((f32[2,1024,1024]{2,1,0:T(8,128)}), f32[2,128,1024]{2,1,0:T(8,128)}) %reduce-scatter.15.cloned.1.call-update) | async-done | bytes 1048592 | tf_op jit(solution)/shard_map/reduce_scatter | solution.py:172
  802.8 3.6 fusion.75
  808.3 72.0 %all-gather.25.cloned.1.call-done = bf16[2,1024,1024]{2,1,0:T(8,128)(2,1)} async-done(((bf16[2,128,1024]{2,1,0:T(8,128)(2,1)}), bf16[2,1024,1024]{2,1,0:T(8,128)(2,1)}) %all-gather.25.cloned.1.call-update) | async-done | bytes 4194320 | tf_op jit(solution)/shard_map/all_gather | solution.py:199
  880.3 3.4 convolution_convert_fusion
  884.9 21.7 %while.23 = (s32[]{:T(128)}, bf16[2,1024,2,192]{1,3,2,0:T(8,128)(2,1)}, bf16[2,1024,2,64]{1,3,2,0:T(8,128)(2,1)S(1)}, bf16[2,1024,2,64]{1,3,2,0:T(8,128)(2,1)S(1...) while((s32[]{:T(128)}, ...), condition=%wide.region_16.17_spmd, body=%wide.region_14.16_spmd.sunk | while | flops 1370355712 | bytes 79751328 | solution.py:209
  886.2 1.6 fusion.149
  887.8 2.0 multiply_reduce_fusion.11
  889.8 2.4 multiply_convert_fusion.9
  893.1 1.4 fusion.150
  897.1 1.6 fusion.149
  898.6 2.0 multiply_reduce_fusion.11
  900.6 2.4 multiply_convert_fusion.9
  903.9 1.4 fusion.150
  906.6 7.0 convolution_bitcast_fusion
  913.7 1.3 copy-done.8
  916.6 6.6 fusion.101
  923.3 7.3 fusion.89
  931.4 3.8 fusion.100
  935.3 1.6 copy.70
  937.6 3.0 fusion.99
  940.6 119.2 %reduce-scatter.19.cloned.1.call-done = f32[2,128,1024]{2,1,0:T(8,128)} async-done(((f32[2,1024,1024]{2,1,0:T(8,128)}), f32[2,128,1024]{2,1,0:T(8,128)}) %reduce-scatter.19.cloned.1.call-update) | async-done | bytes 1048592 | tf_op jit(solution)/shard_map/reduce_scatter | solution.py:221
  1059.8 1.8 fusion.72
  1061.7 35.9 %psum.15 = f32[2,6144]{1,0:T(2,128)S(1)} all-reduce(f32[2,6144]{1,0:T(2,128)S(1)} %constant_dynamic-update-slice_fusion), channel_id=1, replica_groups=mesh['fsdp'=4,'tp'=8] {'tp'}, use_global_device_ids=true, to_apply=%region_26.27 | all-reduce | flops 12288 | bytes 98304 | tf_op jit(solution)/shard_map/psum | solution.py:236
  1097.5 2.3 fusion.80
  1102.4 3.0 convert_reduce_fusion
  1106.6 1.4 copy.82
  1108.0 11.3 all-reduce.4
  1122.9 2.6 fusion.71
  1125.5 24.4 %reduce-scatter.29.cloned.1.call-done = f32[512,256]{1,0:T(8,128)} async-done(((f32[512,1024]{1,0:T(8,128)}), f32[512,256]{1,0:T(8,128)}) %reduce-scatter.29.cloned.1.call-update) | async-done | bytes 524304 | tf_op jit(solution)/shard_map/reduce_scatter | solution.py:250
  1149.9 24.6 %reduce-scatter.25.cloned.1.call-done = f32[128,256]{1,0:T(8,128)} async-done(((f32[128,1024]{1,0:T(8,128)}), f32[128,256]{1,0:T(8,128)}) %reduce-scatter.25.cloned.1.call-update) | async-done | bytes 131088 | tf_op jit(solution)/shard_map/reduce_scatter | solution.py:246
  1174.5 31.1 %reduce-scatter.23.cloned.1.call-done = f32[256,2,192]{0,2,1:T(8,128)} async-done(((f32[1024,2,192]{0,2,1:T(8,128)}), f32[256,2,192]{0,2,1:T(8,128)}) %reduce-scatter.23.cloned.1.call-update) | async-done | bytes 393232 | tf_op jit(solution)/shard_map/reduce_scatter | solution.py:244
  1205.5 40.8 %reduce-scatter.21.cloned.1.call-done = f32[128,1536]{1,0:T(8,128)} async-done(((f32[128,6144]{1,0:T(8,128)}), f32[128,1536]{1,0:T(8,128)}) %reduce-scatter.21.cloned.1.call-update) | async-done | bytes 786448 | tf_op jit(solution)/shard_map/reduce_scatter | solution.py:242
  (167 shorter events, 29.6 us)
Async XLA Ops:
  7.2 67.0 %copy-start.24 = (bf16[2,32]{1,0:T(2,128)(2,1)S(1)}, bf16[2,32]{1,0:T(2,128)(2,1)}, u32[]{:S(2)}) copy-start(bf16[2,32]{1,0:T(2,128)(2,1)} %param.23) | copy-start | bytes 388
  7.2 72.2 %copy-start.18 = (bf16[128,256]{1,0:T(8,128)(2,1)S(1)}, bf16[128,256]{1,0:T(8,128)(2,1)}, u32[]{:S(2)}) copy-start(bf16[128,256]{1,0:T(8,128)(2,1)} %param.24) | copy-start | bytes 196612
  7.2 78.1 %copy-start.15 = (bf16[256,2,192]{0,2,1:T(8,128)(2,1)S(1)}, bf16[256,2,192]{0,2,1:T(8,128)(2,1)}, u32[]{:S(2)}) copy-start(bf16[256,2,192]{0,2,1:T(8,128)(2,1)} %param.22) | copy-start | bytes 589828
  7.2 24.8 %all-gather.13.cloned.1.call-start = ((), (), s32[]{:S(2)}) async-start(), calls=%async_computation.10 | async-start | bytes 1966080 | tf_op jit(solution)/shard_map/all_gather | solution.py:104
  7.9 135.4 %all-gather.15.cloned.1.call-start = ((), (), s32[]{:S(2)}) async-start(), calls=%async_computation.11 | async-start | bytes 4718592 | tf_op jit(solution)/shard_map/all_gather | solution.py:131
  16.1 131.2 %copy-start.19 = (f32[2,128]{1,0:T(2,128)}, f32[2,128]{1,0:T(2,128)S(1)}, u32[]{:S(2)}) copy-start(f32[2,128]{1,0:T(2,128)S(1)} %broadcast_multiply_fusion.5) | copy-start | bytes 3076
  17.5 56.6 %copy-start.21 = (f32[2,128]{1,0:T(2,128)}, f32[2,128]{1,0:T(2,128)S(1)}, u32[]{:S(2)}) copy-start(f32[2,128]{1,0:T(2,128)S(1)} %add_rsqrt_fusion.1) | copy-start | bytes 3076
  71.3 0.6 copy-start.16
  74.1 232.6 %reduce-scatter.13.cloned.1.call-start = ((), (), s32[]{:S(2)}) async-start(), calls=%async_computation.12 | async-start | bytes 9437184 | tf_op jit(solution)/shard_map/reduce_scatter | solution.py:158
  94.0 53.3 %copy-start.13 = (bf16[1024,2,192]{0,2,1:T(8,128)(2,1)}, bf16[1024,2,192]{0,2,1:T(8,128)(2,1)S(1)}, u32[]{:S(2)}) copy-start(bf16[1024,2,192]{0,2,1:T(8,128)(2,1)S(1)} %all_gather.45) | copy-start | bytes 2359300
  156.0 4.5 copy-start.10
  160.6 0.7 copy-start.28
  160.6 146.1 %copy-start = (bf16[2,128,1024]{2,1,0:T(8,128)(2,1)S(1)}, bf16[2,128,1024]{2,1,0:T(8,128)(2,1)}, u32[]{:S(2)}) copy-start(bf16[2,128,1024]{2,1,0:T(8,128)(2,1)} %param.17) | copy-start | bytes 1572868
  160.6 151.6 %copy-start.25 = (bf16[128]{0:T(256)(128)(2,1)S(1)}, bf16[128]{0:T(256)(128)(2,1)}, u32[]{:S(2)}) copy-start(bf16[128]{0:T(256)(128)(2,1)} %param.27) | copy-start | bytes 772
  160.6 163.4 %all-gather.19.cloned.1.call-start = ((), (), s32[]{:S(2)}) async-start(), calls=%async_computation.14 | async-start | bytes 1310720 | tf_op jit(solution)/shard_map/all_gather | solution.py:110
  161.2 238.2 %all-gather.17.cloned.1.call-start = ((), (), s32[]{:S(2)}) async-start(), calls=%async_computation.13 | async-start | bytes 4718592 | tf_op jit(solution)/shard_map/all_gather | solution.py:163
  309.5 106.6 %all-gather.21.cloned.1.call-start = ((), (), s32[]{:S(2)}) async-start(), calls=%async_computation.15 | async-start | bytes 1310720 | tf_op jit(solution)/shard_map/all_gather | solution.py:112
  310.1 181.6 %all-gather.23.cloned.1.call-start = ((), (), s32[]{:S(2)}) async-start(), calls=%async_computation.17 | async-start | bytes 4718592 | tf_op jit(solution)/shard_map/all_gather | solution.py:179
  312.2 340.4 %reduce-scatter.17.cloned.1.call-start = ((), (), s32[]{:S(2)}) async-start(), calls=%async_computation.18 | async-start | bytes 9437184 | tf_op jit(solution)/shard_map/reduce_scatter | solution.py:193
  491.7 9.0 copy-start.27
  500.7 5.6 copy-start.12
  506.4 296.4 %reduce-scatter.15.cloned.1.call-start = ((), (), s32[]{:S(2)}) async-start(), calls=%async_computation.16 | async-start | bytes 9437184 | tf_op jit(solution)/shard_map/reduce_scatter | solution.py:172
  515.0 0.7 copy-start.29
  515.0 287.8 %copy-start.9 = (bf16[2,128,1024]{2,1,0:T(8,128)(2,1)S(1)}, bf16[2,128,1024]{2,1,0:T(8,128)(2,1)}, u32[]{:S(2)}) copy-start(bf16[2,128,1024]{2,1,0:T(8,128)(2,1)} %param.18) | copy-start | bytes 1572868
  515.0 365.3 %all-gather.25.cloned.1.call-start = ((), (), s32[]{:S(2)}) async-start(), calls=%async_computation.19 | async-start | bytes 4718592 | tf_op jit(solution)/shard_map/all_gather | solution.py:199
  806.4 1.0 copy-start.3
  808.2 251.5 %reduce-scatter.19.cloned.1.call-start = ((), (), s32[]{:S(2)}) async-start(), calls=%async_computation.20 | async-start | bytes 9437184 | tf_op jit(solution)/shard_map/reduce_scatter | solution.py:221
  884.9 21.7 %copy-start.14 = (bf16[1024,2,192]{0,2,1:T(8,128)(2,1)S(1)}, bf16[1024,2,192]{0,2,1:T(8,128)(2,1)}, u32[]{:S(2)}) copy-start(bf16[1024,2,192]{0,2,1:T(8,128)(2,1)} %copy-done.13) | copy-start | bytes 2359300
  892.2 2.3 copy-start.6
  894.6 1.2 copy-start.7
  903.1 2.3 copy-start.6
  905.4 1.2 copy-start.7
  913.6 1.4 copy-start.8
  913.6 192.9 %reduce-scatter.31.cloned.1.call-start = ((), (), s32[]{:S(2)}) async-start(), calls=%async_computation.26 | async-start | bytes 81920
  916.2 209.3 %reduce-scatter.27.cloned.1.call-start = ((), (), s32[]{:S(2)}) async-start(), calls=%async_computation.24 | async-start | bytes 2621440 | tf_op jit(solution)/shard_map/reduce_scatter | solution.py:248
  923.3 7.5 copy-start.11
  923.3 226.6 %reduce-scatter.29.cloned.1.call-start = ((), (), s32[]{:S(2)}) async-start(), calls=%async_computation.25 | async-start | bytes 2621440 | tf_op jit(solution)/shard_map/reduce_scatter | solution.py:250
  930.7 243.8 %reduce-scatter.25.cloned.1.call-start = ((), (), s32[]{:S(2)}) async-start(), calls=%async_computation.23 | async-start | bytes 655360 | tf_op jit(solution)/shard_map/reduce_scatter | solution.py:246
  935.3 270.3 %reduce-scatter.23.cloned.1.call-start = ((), (), s32[]{:S(2)}) async-start(), calls=%async_computation.22 | async-start | bytes 1966080 | tf_op jit(solution)/shard_map/reduce_scatter | solution.py:244
  935.3 2.2 copy-start.26
  937.5 122.3 %copy-start.1 = (bf16[2,128,1024]{2,1,0:T(8,128)(2,1)S(1)}, bf16[2,128,1024]{2,1,0:T(8,128)(2,1)}, u32[]{:S(2)}) copy-start(bf16[2,128,1024]{2,1,0:T(8,128)(2,1)} %param.17) | copy-start | bytes 1572868
  937.5 122.3 %copy-start.17 = (f32[2,1024]{1,0:T(2,128)S(1)}, f32[2,1024]{1,0:T(2,128)}, u32[]{:S(2)}) copy-start(f32[2,1024]{1,0:T(2,128)} %copy-done.16) | copy-start | bytes 24580
  937.5 122.3 %copy-start.20 = (f32[2,128]{1,0:T(2,128)S(1)}, f32[2,128]{1,0:T(2,128)}, u32[]{:S(2)}) copy-start(f32[2,128]{1,0:T(2,128)} %copy-done.19) | copy-start | bytes 3076
  937.5 122.3 %copy-start.22 = (f32[2,128]{1,0:T(2,128)S(1)}, f32[2,128]{1,0:T(2,128)}, u32[]{:S(2)}) copy-start(f32[2,128]{1,0:T(2,128)} %copy-done.21) | copy-start | bytes 3076
  937.5 160.0 %copy-start.23 = (f32[2,128]{1,0:T(2,128)S(1)}, f32[2,128]{1,0:T(2,128)}, u32[]{:S(2)}) copy-start(f32[2,128]{1,0:T(2,128)} %param.19) | copy-start | bytes 3076
  940.5 159.3 %copy-start.30 = (u32[32]{0:T(128)S(1)}, u32[32]{0:T(128)}, u32[]{:S(2)}) copy-start(u32[32]{0:T(128)} %constant.80) | copy-start | bytes 388
  940.6 305.7 %reduce-scatter.21.cloned.1.call-start = ((), (), s32[]{:S(2)}) async-start(), calls=%async_computation.21 | async-start | bytes 3932160 | tf_op jit(solution)/shard_map/reduce_scatter | solution.py:242
  1102.4 3.5 copy-start.2
  1102.4 19.4 %copy-start.5 = (bf16[128,6144]{1,0:T(8,128)(2,1)S(1)}, bf16[128,6144]{1,0:T(8,128)(2,1)}, u32[]{:S(2)}) copy-start(bf16[128,6144]{1,0:T(8,128)(2,1)} %all-gather.13.cloned.1.call-done) | copy-start | bytes 4718596
  1102.4 20.5 %copy-start.4 = (f32[2,128,1024]{2,1,0:T(8,128)S(1)}, f32[2,128,1024]{2,1,0:T(8,128)}, u32[]{:S(2)}) copy-start(f32[2,128,1024]{2,1,0:T(8,128)} %copy-done.3) | copy-start | bytes 3145732
Sparse Core Ops, SparseCore 0:
  9.6 22.3 all-gather.12
  74.2 69.0 all-gather.14
  160.7 145.9 reduce-scatter.12
  308.1 15.7 all-gather.18
  326.6 72.7 all-gather.16
  400.8 15.3 all-gather.20
  418.9 72.7 all-gather.22
  506.5 145.9 reduce-scatter.16
  656.2 146.5 reduce-scatter.14
  808.4 71.8 all-gather.24
  913.8 145.9 reduce-scatter.18
  1062.1 18.6 reduce-scatter.30
  1083.9 31.3 reduce-scatter.26
  1118.3 31.5 reduce-scatter.28
  1152.8 21.6 reduce-scatter.24
  1177.4 28.0 reduce-scatter.22
  1208.5 37.7 reduce-scatter.20
where the time goes:
time: 1260 us; the launch traced here: 1250 us
  waiting for transfers between devices  966 us (77%)
  blocking collectives  126 us (10%)
  matrix products  94.7 us (8%)
  other arithmetic  32.1 us (3%)
  between operations  16.6 us (1%)
  local copies, waits for them, and re-layouts  16.5 us (1%)
    reduce_scatter x1, waiting for transfers between devices, on_device(): lax.psum_scatter(mlp_terms, 'tp', scatter_dimension=1, tiled=True)  148 us
    reduce_scatter x1, waiting for transfers between devices, on_device(): lax.psum_scatter(attn_terms, 'tp', scatter_dimension=1, tiled=True)  140 us
    reduce_scatter x1, waiting for transfers between devices, on_device(): lax.psum_scatter(mlp_in_terms, 'tp', scatter_dimension=1, tiled=True)  132 us
    reduce_scatter x1, waiting for transfers between devices, on_device(): lax.psum_scatter(attn_in_terms, 'tp', scatter_dimension=1, tiled=True)  119 us
    all_gather x1, waiting for transfers between devices, on_device(): lax.all_gather(grad_mlp_out, 'tp', axis=1, tiled=True)  75.6 us
    all_gather x1, waiting for transfers between devices, on_device(): mlp_rows = lax.all_gather(mlp_local, 'tp', axis=1, tiled=True)  75.4 us
    all_gather x1, waiting for transfers between devices, on_device(): lax.all_gather(grad_attn_out, 'tp', axis=1, tiled=True)  72 us
    all_gather x1, waiting for transfers between devices, on_device(): attn_rows = lax.all_gather(attn_local, 'tp', axis=1, tiled=True)  49.3 us
  transfers between devices with their start and end apart: 17, of which 15 were waited for; matrix products, arithmetic and copies ran while one was open for 5% of the time, Pallas kernels for 0%

commit v1 on v0

--- a/solution.py
+++ b/solution.py
@@ -233,7 +233,10 @@
         ],
         -1,
     )
-    grad_modulation = lax.psum(mod_terms, "tp")
+    count, grad_modulation = (lax.axis_size("tp"), mod_terms)
+    for far in [1 << k for k in range(count.bit_length() - 1)]:
+        swap = [(i, i ^ far) for i in range(count)]
+        grad_modulation = grad_modulation + lax.ppermute(grad_modulation, "tp", swap)
     grad_mod_low = grad_modulation.astype(jnp.bfloat16)
     grad_mod_w = jnp.dot(cond_low.T, grad_mod_low, preferred_element_type=jnp.float32)
     grad_mod_bias = jnp.sum(grad_modulation, 0)

time: 1260 us -> 1260 us (level)
  blocking collectives: 126 us -> 89.2 us
  waiting for transfers between devices: 966 us -> 998 us
    psum x1 -> x0, blocking collectives: 35.9 us -> none  [on_device(): grad_modulation = lax.psum(mod_terms, 'tp')]
  transfers between devices with their start and end apart: 17 -> 20, of which waited for: 15 -> 19; matrix products, arithmetic and copies ran while one was open for 5% -> 5% of each run, Pallas kernels for 0% -> 0%
where the time goes in v1:
time: 1260 us; the launch traced here: 1250 us
  waiting for transfers between devices  998 us (79%)
  matrix products  94.7 us (8%)
  blocking collectives  89.2 us (7%)
  other arithmetic  32.1 us (3%)
  between operations  16.6 us (1%)
  local copies, waits for them, and re-layouts  16.5 us (1%)
    reduce_scatter x1, waiting for transfers between devices, on_device(): lax.psum_scatter(mlp_terms, 'tp', scatter_dimension=1, tiled=True)  148 us
    reduce_scatter x1, waiting for transfers between devices, on_device(): lax.psum_scatter(attn_terms, 'tp', scatter_dimension=1, tiled=True)  140 us
    reduce_scatter x1, waiting for transfers between devices, on_device(): lax.psum_scatter(mlp_in_terms, 'tp', scatter_dimension=1, tiled=True)  132 us
    reduce_scatter x1, waiting for transfers between devices, on_device(): lax.psum_scatter(attn_in_terms, 'tp', scatter_dimension=1, tiled=True)  119 us
    all_gather x1, waiting for transfers between devices, on_device(): lax.all_gather(grad_mlp_out, 'tp', axis=1, tiled=True)  75.6 us
    all_gather x1, waiting for transfers between devices, on_device(): mlp_rows = lax.all_gather(mlp_local, 'tp', axis=1, tiled=True)  75.4 us
    all_gather x1, waiting for transfers between devices, on_device(): lax.all_gather(grad_attn_out, 'tp', axis=1, tiled=True)  72 us
    all_gather x1, waiting for transfers between devices, on_device(): attn_rows = lax.all_gather(attn_local, 'tp', axis=1, tiled=True)  49.3 us
  transfers between devices with their start and end apart: 20, of which 19 were waited for; matrix products, arithmetic and copies ran while one was open for 5% of the time, Pallas kernels for 0%

profile of v1, /device:TPU:0, one launch (start us, length us, event | category | flops | bytes accessed | tf_op | source)
XLA Modules:
  0.0 1252.4 jit_solution(18168867390697138303)
XLA Ops:
  8.7 6.2 all-gather
  17.5 14.5 %all-gather.13.cloned.1.call-done = bf16[128,6144]{1,0:T(8,128)(2,1)} async-done(((bf16[128,1536]{1,0:T(8,128)(2,1)}), bf16[128,6144]{1,0:T(8,128)(2,1)}) %all-gather.13.cloned.1.call-update) | async-done | bytes 1572880 | tf_op jit(solution)/shard_map/all_gather | solution.py:104
  32.0 1.7 fusion.83
  33.7 37.5 %psum.7 = f32[2,6144]{1,0:T(2,128)S(1)} all-reduce(f32[2,6144]{1,0:T(2,128)S(1)} %fusion.83), channel_id=1, replica_groups=mesh['fsdp'=4,'tp'=8] {'tp'}, use_global_device_ids=true, to_apply=%region_0.1 | all-reduce | flops 12288 | bytes 98304 | tf_op jit(solution)/shard_map/psum | solution.py:119
  71.9 2.1 fusion.67
  74.1 5.1 all-gather.1
  79.4 5.8 all_gather.47
  85.3 8.7 all_gather.45
  94.0 49.3 %all-gather.15.cloned.1.call-done = bf16[2,1024,1024]{2,1,0:T(8,128)(2,1)} async-done(((bf16[2,128,1024]{2,1,0:T(8,128)(2,1)}), bf16[2,1024,1024]{2,1,0:T(8,128)(2,1)}) %all-gather.15.cloned.1.call-update) | async-done | bytes 4194320 | tf_op jit(solution)/shard_map/all_gather | solution.py:131
  143.3 4.0 add_convert_fusion
  147.5 8.6 while.22
  150.2 1.5 fusion.136
  154.5 1.5 fusion.136
  156.0 4.5 fusion.78
  161.2 5.1 all-gather.2
  166.3 140.4 %reduce-scatter.13.cloned.1.call-done = f32[2,128,1024]{2,1,0:T(8,128)} async-done(((f32[2,1024,1024]{2,1,0:T(8,128)}), f32[2,128,1024]{2,1,0:T(8,128)}) %reduce-scatter.13.cloned.1.call-update) | async-done | bytes 1048592 | tf_op jit(solution)/shard_map/reduce_scatter | solution.py:158
  306.7 1.5 fusion.87
  310.2 2.0 fusion.74
  312.2 5.2 all-gather.3
  317.5 6.5 all-gather.19.cloned.1.call-done
  324.0 75.4 %all-gather.17.cloned.1.call-done = bf16[2,1024,1024]{2,1,0:T(8,128)(2,1)} async-done(((bf16[2,128,1024]{2,1,0:T(8,128)(2,1)}), bf16[2,1024,1024]{2,1,0:T(8,128)(2,1)}) %all-gather.17.cloned.1.call-update) | async-done | bytes 4194320 | tf_op jit(solution)/shard_map/all_gather | solution.py:163
  399.4 6.8 fusion.92
  406.1 10.0 all-gather.21.cloned.1.call-done
  416.2 75.6 %all-gather.23.cloned.1.call-done = bf16[2,1024,1024]{2,1,0:T(8,128)(2,1)} async-done(((bf16[2,128,1024]{2,1,0:T(8,128)(2,1)}), bf16[2,1024,1024]{2,1,0:T(8,128)(2,1)}) %all-gather.23.cloned.1.call-update) | async-done | bytes 4194320 | tf_op jit(solution)/shard_map/all_gather | solution.py:179
  491.7 9.0 convert_reduce_fusion.2
  500.7 5.6 fusion.93
  506.4 8.6 fusion.85
  515.6 5.1 all-gather.4
  520.7 131.8 %reduce-scatter.17.cloned.1.call-done = f32[2,128,1024]{2,1,0:T(8,128)} async-done(((f32[2,1024,1024]{2,1,0:T(8,128)}), f32[2,128,1024]{2,1,0:T(8,128)}) %reduce-scatter.17.cloned.1.call-update) | async-done | bytes 1048592 | tf_op jit(solution)/shard_map/reduce_scatter | solution.py:193
  652.5 1.7 multiply_reduce_fusion.2
  654.3 148.5 %reduce-scatter.15.cloned.1.call-done = f32[2,128,1024]{2,1,0:T(8,128)} async-done(((f32[2,1024,1024]{2,1,0:T(8,128)}), f32[2,128,1024]{2,1,0:T(8,128)}) %reduce-scatter.15.cloned.1.call-update) | async-done | bytes 1048592 | tf_op jit(solution)/shard_map/reduce_scatter | solution.py:172
  802.8 3.6 fusion.75
  808.3 72.0 %all-gather.25.cloned.1.call-done = bf16[2,1024,1024]{2,1,0:T(8,128)(2,1)} async-done(((bf16[2,128,1024]{2,1,0:T(8,128)(2,1)}), bf16[2,1024,1024]{2,1,0:T(8,128)(2,1)}) %all-gather.25.cloned.1.call-update) | async-done | bytes 4194320 | tf_op jit(solution)/shard_map/all_gather | solution.py:199
  880.3 3.4 convolution_convert_fusion
  884.9 21.7 %while.23 = (s32[]{:T(128)}, bf16[2,1024,2,192]{1,3,2,0:T(8,128)(2,1)}, bf16[2,1024,2,64]{1,3,2,0:T(8,128)(2,1)S(1)}, bf16[2,1024,2,64]{1,3,2,0:T(8,128)(2,1)S(1...) while((s32[]{:T(128)}, ...), condition=%wide.region_16.17_spmd, body=%wide.region_14.16_spmd.sunk | while | flops 1370355712 | bytes 79751328 | solution.py:209
  886.2 1.6 fusion.146
  887.8 2.0 multiply_reduce_fusion.11
  889.8 2.4 multiply_convert_fusion.9
  893.1 1.4 fusion.147
  897.1 1.6 fusion.146
  898.6 2.0 multiply_reduce_fusion.11
  900.6 2.4 multiply_convert_fusion.9
  906.6 7.0 convolution_bitcast_fusion
  916.6 6.6 fusion.96
  923.3 7.3 fusion.84
  931.4 3.8 fusion.95
  935.3 1.6 copy.70
  937.5 3.0 fusion.94
  940.8 119.0 %reduce-scatter.19.cloned.1.call-done = f32[2,128,1024]{2,1,0:T(8,128)} async-done(((f32[2,1024,1024]{2,1,0:T(8,128)}), f32[2,128,1024]{2,1,0:T(8,128)}) %reduce-scatter.19.cloned.1.call-update) | async-done | bytes 1048592 | tf_op jit(solution)/shard_map/reduce_scatter | solution.py:221
  1059.8 1.8 fusion.72
  1061.7 1.5 collective-permute-start
  1063.2 2.6 collective-permute-done
  1066.4 3.6 collective-permute-done.1
  1070.0 1.9 collective-permute-start.2
  1071.9 3.6 collective-permute-done.2
  1075.6 2.3 fusion.82
  1080.5 3.0 convert_reduce_fusion
  1086.0 2.6 fusion.71
  1088.6 10.5 all-reduce.4
  1102.7 12.5 reduce-scatter.27.cloned.1.call-done
  1115.1 34.1 %reduce-scatter.29.cloned.1.call-done = f32[512,256]{1,0:T(8,128)} async-done(((f32[512,1024]{1,0:T(8,128)}), f32[512,256]{1,0:T(8,128)}) %reduce-scatter.29.cloned.1.call-update) | async-done | bytes 524304 | tf_op jit(solution)/shard_map/reduce_scatter | solution.py:253
  1149.3 24.6 %reduce-scatter.25.cloned.1.call-done = f32[128,256]{1,0:T(8,128)} async-done(((f32[128,1024]{1,0:T(8,128)}), f32[128,256]{1,0:T(8,128)}) %reduce-scatter.25.cloned.1.call-update) | async-done | bytes 131088 | tf_op jit(solution)/shard_map/reduce_scatter | solution.py:249
  1173.8 31.1 %reduce-scatter.23.cloned.1.call-done = f32[256,2,192]{0,2,1:T(8,128)} async-done(((f32[1024,2,192]{0,2,1:T(8,128)}), f32[256,2,192]{0,2,1:T(8,128)}) %reduce-scatter.23.cloned.1.call-update) | async-done | bytes 393232 | tf_op jit(solution)/shard_map/reduce_scatter | solution.py:247
  1204.9 40.8 %reduce-scatter.21.cloned.1.call-done = f32[128,1536]{1,0:T(8,128)} async-done(((f32[128,6144]{1,0:T(8,128)}), f32[128,1536]{1,0:T(8,128)}) %reduce-scatter.21.cloned.1.call-update) | async-done | bytes 786448 | tf_op jit(solution)/shard_map/reduce_scatter | solution.py:245
  (174 shorter events, 37.2 us)
Async XLA Ops:
  7.2 67.0 %copy-start.24 = (bf16[2,32]{1,0:T(2,128)(2,1)S(1)}, bf16[2,32]{1,0:T(2,128)(2,1)}, u32[]{:S(2)}) copy-start(bf16[2,32]{1,0:T(2,128)(2,1)} %param.23) | copy-start | bytes 388
  7.2 72.2 %copy-start.18 = (bf16[128,256]{1,0:T(8,128)(2,1)S(1)}, bf16[128,256]{1,0:T(8,128)(2,1)}, u32[]{:S(2)}) copy-start(bf16[128,256]{1,0:T(8,128)(2,1)} %param.24) | copy-start | bytes 196612
  7.2 78.1 %copy-start.15 = (bf16[256,2,192]{0,2,1:T(8,128)(2,1)S(1)}, bf16[256,2,192]{0,2,1:T(8,128)(2,1)}, u32[]{:S(2)}) copy-start(bf16[256,2,192]{0,2,1:T(8,128)(2,1)} %param.22) | copy-start | bytes 589828
  7.2 24.8 %all-gather.13.cloned.1.call-start = ((), (), s32[]{:S(2)}) async-start(), calls=%async_computation.10 | async-start | bytes 1966080 | tf_op jit(solution)/shard_map/all_gather | solution.py:104
  7.9 135.4 %all-gather.15.cloned.1.call-start = ((), (), s32[]{:S(2)}) async-start(), calls=%async_computation.11 | async-start | bytes 4718592 | tf_op jit(solution)/shard_map/all_gather | solution.py:131
  16.1 131.2 %copy-start.19 = (f32[2,128]{1,0:T(2,128)}, f32[2,128]{1,0:T(2,128)S(1)}, u32[]{:S(2)}) copy-start(f32[2,128]{1,0:T(2,128)S(1)} %broadcast_multiply_fusion.5) | copy-start | bytes 3076
  17.5 56.6 %copy-start.21 = (f32[2,128]{1,0:T(2,128)}, f32[2,128]{1,0:T(2,128)S(1)}, u32[]{:S(2)}) copy-start(f32[2,128]{1,0:T(2,128)S(1)} %add_rsqrt_fusion.1) | copy-start | bytes 3076
  71.3 0.6 copy-start.16
  74.1 232.7 %reduce-scatter.13.cloned.1.call-start = ((), (), s32[]{:S(2)}) async-start(), calls=%async_computation.12 | async-start | bytes 9437184 | tf_op jit(solution)/shard_map/reduce_scatter | solution.py:158
  94.0 53.3 %copy-start.13 = (bf16[1024,2,192]{0,2,1:T(8,128)(2,1)}, bf16[1024,2,192]{0,2,1:T(8,128)(2,1)S(1)}, u32[]{:S(2)}) copy-start(bf16[1024,2,192]{0,2,1:T(8,128)(2,1)S(1)} %all_gather.45) | copy-start | bytes 2359300
  156.0 4.5 copy-start.10
  160.6 0.7 copy-start.28
  160.6 146.2 %copy-start = (bf16[2,128,1024]{2,1,0:T(8,128)(2,1)S(1)}, bf16[2,128,1024]{2,1,0:T(8,128)(2,1)}, u32[]{:S(2)}) copy-start(bf16[2,128,1024]{2,1,0:T(8,128)(2,1)} %param.17) | copy-start | bytes 1572868
  160.6 151.7 %copy-start.25 = (bf16[128]{0:T(256)(128)(2,1)S(1)}, bf16[128]{0:T(256)(128)(2,1)}, u32[]{:S(2)}) copy-start(bf16[128]{0:T(256)(128)(2,1)} %param.27) | copy-start | bytes 772
  160.6 163.4 %all-gather.19.cloned.1.call-start = ((), (), s32[]{:S(2)}) async-start(), calls=%async_computation.14 | async-start | bytes 1310720 | tf_op jit(solution)/shard_map/all_gather | solution.py:110
  161.2 238.2 %all-gather.17.cloned.1.call-start = ((), (), s32[]{:S(2)}) async-start(), calls=%async_computation.13 | async-start | bytes 4718592 | tf_op jit(solution)/shard_map/all_gather | solution.py:163
  309.6 106.6 %all-gather.21.cloned.1.call-start = ((), (), s32[]{:S(2)}) async-start(), calls=%async_computation.15 | async-start | bytes 1310720 | tf_op jit(solution)/shard_map/all_gather | solution.py:112
  310.2 181.6 %all-gather.23.cloned.1.call-start = ((), (), s32[]{:S(2)}) async-start(), calls=%async_computation.17 | async-start | bytes 4718592 | tf_op jit(solution)/shard_map/all_gather | solution.py:179
  312.2 340.3 %reduce-scatter.17.cloned.1.call-start = ((), (), s32[]{:S(2)}) async-start(), calls=%async_computation.18 | async-start | bytes 9437184 | tf_op jit(solution)/shard_map/reduce_scatter | solution.py:193
  491.7 9.0 copy-start.27
  500.7 5.6 copy-start.12
  506.4 296.4 %reduce-scatter.15.cloned.1.call-start = ((), (), s32[]{:S(2)}) async-start(), calls=%async_computation.16 | async-start | bytes 9437184 | tf_op jit(solution)/shard_map/reduce_scatter | solution.py:172
  515.0 0.7 copy-start.29
  515.0 287.8 %copy-start.9 = (bf16[2,128,1024]{2,1,0:T(8,128)(2,1)S(1)}, bf16[2,128,1024]{2,1,0:T(8,128)(2,1)}, u32[]{:S(2)}) copy-start(bf16[2,128,1024]{2,1,0:T(8,128)(2,1)} %param.18) | copy-start | bytes 1572868
  515.0 365.3 %all-gather.25.cloned.1.call-start = ((), (), s32[]{:S(2)}) async-start(), calls=%async_computation.19 | async-start | bytes 4718592 | tf_op jit(solution)/shard_map/all_gather | solution.py:199
  806.4 1.0 copy-start.3
  808.3 251.5 %reduce-scatter.19.cloned.1.call-start = ((), (), s32[]{:S(2)}) async-start(), calls=%async_computation.20 | async-start | bytes 9437184 | tf_op jit(solution)/shard_map/reduce_scatter | solution.py:221
  884.9 21.7 %copy-start.14 = (bf16[1024,2,192]{0,2,1:T(8,128)(2,1)S(1)}, bf16[1024,2,192]{0,2,1:T(8,128)(2,1)}, u32[]{:S(2)}) copy-start(bf16[1024,2,192]{0,2,1:T(8,128)(2,1)} %copy-done.13) | copy-start | bytes 2359300
  892.2 2.3 copy-start.6
  894.6 1.2 copy-start.7
  903.1 2.3 copy-start.6
  905.4 1.2 copy-start.7
  913.6 1.4 copy-start.8
  913.6 171.0 %reduce-scatter.31.cloned.1.call-start = ((), (), s32[]{:S(2)}) async-start(), calls=%async_computation.26 | async-start | bytes 81920
  916.2 199.0 %reduce-scatter.27.cloned.1.call-start = ((), (), s32[]{:S(2)}) async-start(), calls=%async_computation.24 | async-start | bytes 2621440 | tf_op jit(solution)/shard_map/reduce_scatter | solution.py:251
  923.3 7.5 copy-start.11
  923.3 226.0 %reduce-scatter.29.cloned.1.call-start = ((), (), s32[]{:S(2)}) async-start(), calls=%async_computation.25 | async-start | bytes 2621440 | tf_op jit(solution)/shard_map/reduce_scatter | solution.py:253
  930.7 243.2 %reduce-scatter.25.cloned.1.call-start = ((), (), s32[]{:S(2)}) async-start(), calls=%async_computation.23 | async-start | bytes 655360 | tf_op jit(solution)/shard_map/reduce_scatter | solution.py:249
  935.2 269.7 %reduce-scatter.23.cloned.1.call-start = ((), (), s32[]{:S(2)}) async-start(), calls=%async_computation.22 | async-start | bytes 1966080 | tf_op jit(solution)/shard_map/reduce_scatter | solution.py:247
  935.3 2.2 copy-start.26
  937.5 122.3 %copy-start.1 = (bf16[2,128,1024]{2,1,0:T(8,128)(2,1)S(1)}, bf16[2,128,1024]{2,1,0:T(8,128)(2,1)}, u32[]{:S(2)}) copy-start(bf16[2,128,1024]{2,1,0:T(8,128)(2,1)} %param.17) | copy-start | bytes 1572868
  937.5 122.3 %copy-start.17 = (f32[2,1024]{1,0:T(2,128)S(1)}, f32[2,1024]{1,0:T(2,128)}, u32[]{:S(2)}) copy-start(f32[2,1024]{1,0:T(2,128)} %copy-done.16) | copy-start | bytes 24580
  937.5 122.3 %copy-start.20 = (f32[2,128]{1,0:T(2,128)S(1)}, f32[2,128]{1,0:T(2,128)}, u32[]{:S(2)}) copy-start(f32[2,128]{1,0:T(2,128)} %copy-done.19) | copy-start | bytes 3076
  937.5 122.3 %copy-start.22 = (f32[2,128]{1,0:T(2,128)S(1)}, f32[2,128]{1,0:T(2,128)}, u32[]{:S(2)}) copy-start(f32[2,128]{1,0:T(2,128)} %copy-done.21) | copy-start | bytes 3076
  937.5 138.1 %copy-start.23 = (f32[2,128]{1,0:T(2,128)S(1)}, f32[2,128]{1,0:T(2,128)}, u32[]{:S(2)}) copy-start(f32[2,128]{1,0:T(2,128)} %param.19) | copy-start | bytes 3076
  940.5 137.4 %copy-start.30 = (u32[32]{0:T(128)S(1)}, u32[32]{0:T(128)}, u32[]{:S(2)}) copy-start(u32[32]{0:T(128)} %constant.80) | copy-start | bytes 388
  940.6 305.1 %reduce-scatter.21.cloned.1.call-start = ((), (), s32[]{:S(2)}) async-start(), calls=%async_computation.21 | async-start | bytes 3932160 | tf_op jit(solution)/shard_map/reduce_scatter | solution.py:245
  1061.7 4.2 collective-permute-start
  1065.8 4.2 collective-permute-start.1
  1070.0 5.5 collective-permute-start.2
  1080.5 3.5 copy-start.2
  1080.5 5.5 copy-start.4
  1083.9 17.7 %copy-start.5 = (bf16[128,6144]{1,0:T(8,128)(2,1)S(1)}, bf16[128,6144]{1,0:T(8,128)(2,1)}, u32[]{:S(2)}) copy-start(bf16[128,6144]{1,0:T(8,128)(2,1)} %all-gather.13.cloned.1.call-done) | copy-start | bytes 4718596
Sparse Core Ops, SparseCore 0:
  9.6 22.3 all-gather.12
  74.2 69.0 all-gather.14
  160.7 145.9 reduce-scatter.12
  308.1 15.7 all-gather.18
  326.6 72.7 all-gather.16
  400.8 15.3 all-gather.20
  418.9 72.7 all-gather.22
  506.5 145.9 reduce-scatter.16
  656.2 146.5 reduce-scatter.14
  808.4 71.8 all-gather.24
  913.8 145.9 reduce-scatter.18
  1062.1 18.6 reduce-scatter.30
  1083.9 31.2 reduce-scatter.26
  1118.1 31.1 reduce-scatter.28
  1152.2 21.6 reduce-scatter.24
  1176.8 28.0 reduce-scatter.22
  1207.9 37.7 reduce-scatter.20
